TPU v7x, 32 devices: a whole 2x2x4 slice. The times are simulated.
32 devices in a mesh: grp: 4 (over y, core), blk: 8 (over z, x).
Axes of the slice: x: 2, y: 2, z: 4, core: 2. Of those that a mesh axis runs over, the one named last changes fastest.
Arguments:
- features: bfloat16 [4096, 128], P(('grp', 'blk')), may hold values from -6 to 6
- col_scale: float32 [4096], P(('grp', 'blk')), may hold values from 0.5 to 2
- row_scale: float32 [4096], P(('grp', 'blk')), may hold values from 0.5 to 2
- tiles: bfloat16 [1024, 128, 128], P(('grp', 'blk')), may hold values from 0 to 0.03125
- tile_cols: int32 [1024], P(('grp', 'blk')), may hold values from 0 to 3
- weight: bfloat16 [128, 256], replicated, may hold values from -0.5 to 0.5
- cotangent: bfloat16 [4096, 256], P(('grp', 'blk')), may hold values from -0.1875 to 0.1875
- train_mask: int32 [4096], P(('grp', 'blk')), may hold values 0 or 1
Outputs:
- hidden: bfloat16 [4096, 256], P(('grp', 'blk'))
- weight_grad: float32 [128, 256], replicated
All inputs are finite; a program needn't handle non-finite values. No bound on the sum of `train_mask` on one device may be relied on, other than what follows from the above.
Results may differ from a plain program's by a relative error of at most 0.0054.
Values may be sent and summed in bfloat16 or wider, within the bound.
A program may use at most 128 MiB of HBM per device.

v0:
```python
import jax
import jax.numpy as jnp
from jax import lax
from jax.sharding import PartitionSpec as P

TPR = 4


def activate(values):
    return jax.nn.gelu(values, approximate=True)


def shards(features, col_scale, row_scale, tiles, tile_cols, weight, cotangent, train_mask):
    node_dev = features.shape[0]
    fin_width = features.shape[1]
    tile = tiles.shape[1]
    per_dev = node_dev // tile
    grp_count = lax.axis_size("grp")
    blk_count = lax.axis_size("blk")
    scaled = (col_scale[:, None] * features.astype(jnp.float32)).astype(jnp.bfloat16)
    moved_tiles, moved_cols = (
        lax.all_to_all(tiles, "blk", split_axis=0, concat_axis=0, tiled=True),
        lax.all_to_all(tile_cols, "blk", split_axis=0, concat_axis=0, tiled=True),
    )
    everything = lax.all_gather(scaled, ("grp", "blk"), axis=0, tiled=True)
    everything = everything.reshape(grp_count * blk_count * per_dev, tile, fin_width)
    cols_view = moved_cols.reshape(blk_count, per_dev * TPR)
    colset = jnp.arange(blk_count, dtype=jnp.int32)[:, None]
    global_cols = (cols_view // per_dev * blk_count + colset) * per_dev + cols_view % per_dev
    picked = jnp.take(everything, global_cols.reshape(-1), axis=0)
    picked = picked.reshape(blk_count, per_dev, TPR, tile, fin_width)
    piece = moved_tiles.reshape(blk_count, per_dev, TPR, tile, tile)
    aggregate = jnp.einsum("bpkij,bpkjf->pif", piece, picked, preferred_element_type=jnp.float32)
    aggregate = aggregate.reshape(node_dev, fin_width)
    mixed = row_scale[:, None] * aggregate
    pre = jnp.dot(mixed, weight.astype(jnp.float32), precision=lax.Precision.HIGHEST)
    hidden, backward = jax.vjp(activate, pre)
    masked_grad = cotangent.astype(jnp.float32) * train_mask.astype(jnp.float32)[:, None]
    delta = backward(masked_grad)[0]
    local_grad = jnp.dot(mixed.T, delta, precision=lax.Precision.HIGHEST)
    weight_grad = lax.psum(local_grad, ("grp", "blk"))
    return (hidden.astype(jnp.bfloat16), weight_grad)


def solution(mesh):
    in_specs = (
        P(("grp", "blk"), None),
        P(("grp", "blk")),
        P(("grp", "blk")),
        P(("grp", "blk"), None, None),
        P(("grp", "blk")),
        P(),
        P(("grp", "blk"), None),
        P(("grp", "blk")),
    )
    out_specs = (P(("grp", "blk"), None), P())
    return jax.shard_map(shards, mesh=mesh, in_specs=in_specs, out_specs=out_specs, check_vma=False)
```

profile of v0, /device:TPU:0, one launch (start us, length us, event | category | flops | bytes accessed | tf_op | source)
XLA Modules:
  0.0 208.8 jit_solution(1757387805213414297)
XLA Ops:
  7.2 0.0 copy-start
  7.2 0.0 all-gather.2.cloned.1.call-start
  7.2 1.5 multiply_convert_fusion.1
  8.7 0.0 copy-start.1
  8.7 0.0 all-gather.2.cloned.1.call-update
  8.7 0.6 copy-done.1
  9.3 0.1 all_to_all.9
  9.4 13.5 %all_to_all.14 = s32[8,4,1]{1,2,0:T(1,128)S(1)} all-to-all(s32[8,4,1]{1,2,0:T(1,128)S(1)} %bitcast.25), channel_id=1, replica_groups=mesh['grp'=4,'blk'=8] {'blk'}, dimensions={0} | all-to-all | bytes 256 | tf_op jit(solution)/shard_map/all_to_all | solution.py:23
  22.9 3.6 %all-to-all-start.1 = ((bf16[32,128,128]{2,1,0:T(8,128)(2,1)}), bf16[32,128,128]{2,1,0:T(8,128)(2,1)S(1)}, u32[]{:S(2)}, u32[]{:S(2)}) async-start(bf16[32,128,128]{2,1,0:T(8,128)(2,1)} %param.11), calls=%async_computation.1 | async-start | bytes 2097152 | tf_op jit(solution)/shard_map/all_to_all | solution.py:22
  26.5 0.0 all-reduce.2.cloned.1.call-start
  26.6 0.0 copy-start.3
  26.6 0.1 add.82
  26.6 0.6 copy-done.3
  27.2 0.1 mul.98
  27.3 0.1 copy.17
  27.4 0.1 copy.18
  27.5 45.2 %all-gather.2.cloned.1.call-done = bf16[4096,128]{1,0:T(8,128)(2,1)} async-done(((bf16[128,128]{1,0:T(8,128)(2,1)}), bf16[4096,128]{1,0:T(8,128)(2,1)}) %all-gather.2.cloned.1.call-update) | async-done | bytes 1048592 | tf_op jit(solution)/shard_map/all_gather | solution.py:25
  72.8 2.0 gather_fusion
  74.8 0.7 copy.19
  75.4 0.0 all-to-all-done.1
  75.4 0.0 copy-start.4
  75.4 0.6 copy-done.4
  76.1 0.5 fusion
  76.6 0.0 copy-done
  76.6 0.0 copy-start.2
  76.6 0.9 multiply_convert_fusion
  77.5 0.0 copy-done.2
  77.5 1.0 fusion.10
  78.6 0.0 all-reduce.2.cloned.1.call-update
  78.6 121.8 %all-reduce.2.cloned.1.call-done = f32[128,256]{1,0:T(8,128)} async-done(((f32[128,256]{1,0:T(8,128)}), f32[128,256]{1,0:T(8,128)}) %all-reduce.2.cloned.1.call-update) | async-done | bytes 131088 | tf_op jit(solution)/shard_map/psum | solution.py:41
  200.4 1.6 copy.22
  (6 shorter events, 0.0 us)
Async XLA Ops:
  7.2 69.4 %copy-start = (bf16[128,256]{1,0:T(8,128)(2,1)S(1)}, bf16[128,256]{1,0:T(8,128)(2,1)}, u32[]{:S(2)}) copy-start(bf16[128,256]{1,0:T(8,128)(2,1)} %param.13) | copy-start | bytes 196612
  7.2 65.6 %all-gather.2.cloned.1.call-start = ((), (), s32[]{:S(2)}) async-start(), calls=%async_computation.2 | async-start | bytes 1081344 | tf_op jit(solution)/shard_map/all_gather | solution.py:25
  8.7 0.7 copy-start.1
  22.9 52.5 %all-to-all-start.1 = ((bf16[32,128,128]{2,1,0:T(8,128)(2,1)}), bf16[32,128,128]{2,1,0:T(8,128)(2,1)S(1)}, u32[]{:S(2)}, u32[]{:S(2)}) async-start(bf16[32,128,128]{2,1,0:T(8,128)(2,1)} %param.11), calls=%async_computation.1 | async-start | bytes 2097152 | tf_op jit(solution)/shard_map/all_to_all | solution.py:22
  26.5 173.9 %all-reduce.2.cloned.1.call-start = ((), (), s32[]{:S(2)}) async-start(), calls=%async_computation.3 | async-start | bytes 262144 | tf_op jit(solution)/shard_map/psum | solution.py:41
  26.6 0.7 copy-start.3
  75.4 0.7 copy-start.4
  76.6 0.9 copy-start.2
Sparse Core Ops, SparseCore 0:
  11.6 61.1 all-gather.1
  78.9 121.4 all-reduce.1
where the time goes:
time: 209 us
  waiting for transfers between devices  167 us (80%)
  between operations  14.1 us (7%)
  blocking collectives  13.5 us (6%)
  local copies, waits for them, and re-layouts  6.49 us (3%)
  starting transfers between devices  3.64 us (2%)
  matrix products  2.43 us (1%)
    psum x1, waiting for transfers between devices, shards(): weight_grad = lax.psum(local_grad, ('grp', 'blk'))  122 us
    all_gather x1, waiting for transfers between devices, shards(): everything = lax.all_gather(scaled, ('grp', 'blk'), axis=0, tiled=True)  45.2 us
    all_to_all x1, blocking collectives, shards(): lax.all_to_all(tile_cols, 'blk', split_axis=0, concat_axis=0, tiled=True)  13.5 us
  transfers between devices with their start and end apart: 3, of which 2 were waited for; matrix products, arithmetic and copies ran while one was open for 1% of the time, Pallas kernels for 0%

commit v1 on v0

v1 whole, which is shorter than its diff:
```python
import functools
import math

import jax
import jax.numpy as jnp
from jax import lax
from jax.experimental import pallas as pl
from jax.experimental.pallas import tpu as pltpu
from jax.sharding import PartitionSpec as P

TPR = 4
ROOT = math.sqrt(2.0 / math.pi)
CUBE = 0.044715
MESH = pl.DeviceIdType.MESH
F32 = jnp.float32
BF16 = jnp.bfloat16
GRAD_LINK = F32


def far_first(count):
    return sorted(range(1, count), key=lambda step: abs(2 * step - count))


def split(value):
    high = value.astype(BF16)
    return high, (value - high.astype(F32)).astype(BF16)


def down_rows(row, width):
    return jnp.broadcast_to(row, (width, row.shape[1])).T


def kernel(n_grp, n_blk, pieces, cols, features, col_scale, row_scale, tiles, weight, cotangent,
           train_mask, hidden_out, grad_out, feat, cscale, rscale, mask, wgt, cot, held, sources,
           mine, outgoing, arrived, hid, grad_parts, grad_in, grad_all, in_sems, tile_sems, src_send,
           src_recv, part_send, part_recv, grad_sems, out_sems):
    g, b = lax.axis_index("grp"), lax.axis_index("blk")
    order = far_first(n_blk) + [0]

    def grp_peer(step):
        return lax.rem(g + step, n_grp)

    def blk_peer(step):
        return lax.rem(b + step, n_blk)

    def load(source, target, sem):
        copy = pltpu.make_async_copy(source, target, sem)
        copy.start()
        return copy

    first = [load(features, feat, in_sems.at[0]), load(col_scale, cscale, in_sems.at[1])]

    barrier = pltpu.get_barrier_semaphore()
    for step in range(1, n_grp):
        pl.semaphore_signal(barrier, inc=1, device_id=(grp_peer(step), b), device_id_type=MESH)
    for step in range(1, n_blk):
        pl.semaphore_signal(barrier, inc=1, device_id=(g, blk_peer(step)), device_id_type=MESH)

    tile_loads = []
    for spot, step in enumerate(order):
        rows = pl.ds(blk_peer(step) * TPR, TPR)
        tile_loads.append(load(tiles.at[rows], held.at[rows], tile_sems.at[spot]))
    late = [
        load(row_scale, rscale, in_sems.at[2]),
        load(train_mask, mask, in_sems.at[3]),
        load(weight, wgt, in_sems.at[4]),
        load(cotangent, cot, in_sems.at[5]),
    ]

    for copy in first:
        copy.wait()
    sources[g] = (down_rows(cscale[...], feat.shape[1]) * feat[...].astype(F32)).astype(BF16)
    pl.semaphore_wait(barrier, n_grp + n_blk - 2)

    src_copies = []
    for step in range(1, n_grp):
        copy = pltpu.make_async_remote_copy(
            src_ref=sources.at[g], dst_ref=sources.at[g],
            send_sem=src_send.at[step - 1], recv_sem=src_recv.at[step - 1],
            device_id=(grp_peer(step), b), device_id_type=MESH)
        copy.start()
        src_copies.append(copy)
    for copy in tile_loads:
        copy.wait()
    for copy in src_copies:
        copy.wait()

    def partial(block):
        base = block * TPR
        left = jnp.concatenate([held[base + k] for k in range(TPR)], axis=1)
        right = jnp.concatenate([sources[cols[base + k]] for k in range(TPR)], axis=0)
        return jnp.dot(left, right, preferred_element_type=F32)

    part_copies = []
    for spot, step in enumerate(order[:-1]):
        block = blk_peer(step)
        outgoing[spot] = partial(block).astype(BF16)
        copy = pltpu.make_async_remote_copy(
            src_ref=outgoing.at[spot], dst_ref=arrived.at[spot],
            send_sem=part_send.at[spot], recv_sem=part_recv.at[spot],
            device_id=(g, block), device_id_type=MESH)
        copy.start()
        part_copies.append(copy)
    mine[...] = partial(b)

    for copy in late:
        copy.wait()
    row_full = down_rows(rscale[...], feat.shape[1])
    mask_full = down_rows(mask[...].astype(F32), cot.shape[1] // 2)
    masked = cot[...].astype(F32) * jnp.concatenate([mask_full, mask_full], axis=1)

    total = mine[...]
    for spot, copy in reversed(list(enumerate(part_copies))):
        copy.wait()
        total = total + arrived[spot].astype(F32)
    mixed = row_full * total

    high, low = split(mixed)
    w = wgt[...]
    pre = jnp.dot(jnp.concatenate([high, low], axis=1), jnp.concatenate([w, w], axis=0),
                  preferred_element_type=F32)
    square = pre * pre
    bent = jnp.tanh(ROOT * pre * (1.0 + CUBE * square))
    half = 0.5 * (1.0 + bent)
    hid[...] = (pre * half).astype(BF16)
    out_copy = load(hid, hidden_out, out_sems.at[0])
    slope = half + 0.5 * pre * (1.0 - bent * bent) * (ROOT * (1.0 + 3.0 * CUBE * square))
    delta = slope * masked

    high_t, low_t = split(mixed.T)
    d_high, d_low = split(delta)
    grad = jnp.dot(jnp.concatenate([high_t, low_t, high_t], axis=1),
                   jnp.concatenate([d_high, d_high, d_low], axis=0), preferred_element_type=F32)
    if not pieces:
        grad_all[...] = grad
        load(grad_all, grad_out, out_sems.at[1]).wait()
        out_copy.wait()
        return

    n = n_grp * n_blk
    me = g * n_blk + b
    wide = grad.shape[1] // 128
    for piece in range(n):
        at, lane = piece // wide * 8, piece % wide * 128
        grad_parts[piece] = grad[at:at + 8, lane:lane + 128].astype(GRAD_LINK)

    def scatter(step, _):
        to = lax.rem(me + step, n)
        pltpu.make_async_remote_copy(
            src_ref=grad_parts.at[to], dst_ref=grad_in.at[n - 1 - step],
            send_sem=grad_sems.at[0], recv_sem=grad_sems.at[1],
            device_id=(to // n_blk, lax.rem(to, n_blk)), device_id_type=MESH).start()
        return 0

    lax.fori_loop(1, n, scatter, 0)
    some = grad_parts.at[pl.ds(0, n - 1)]
    pltpu.make_async_copy(grad_in, grad_in, grad_sems.at[1]).wait()
    summed = grad_parts[me].astype(F32) + jnp.sum(grad_in[...].astype(F32), axis=0)
    grad_all[me] = summed.astype(GRAD_LINK)

    def gather(step, _):
        to = lax.rem(me + step, n)
        pltpu.make_async_remote_copy(
            src_ref=grad_all.at[me], dst_ref=grad_all.at[me],
            send_sem=grad_sems.at[2], recv_sem=grad_sems.at[3],
            device_id=(to // n_blk, lax.rem(to, n_blk)), device_id_type=MESH).start()
        return 0

    lax.fori_loop(1, n, gather, 0)
    pltpu.make_async_copy(some, some, grad_sems.at[0]).wait()
    pltpu.make_async_copy(some, some, grad_sems.at[2]).wait()
    pltpu.make_async_copy(some, some, grad_sems.at[3]).wait()
    for piece in range(n):
        at, lane = piece // wide * 8, piece % wide * 128
        grad_out[at:at + 8, lane:lane + 128] = grad_all[piece].astype(F32)
    out_copy.wait()


def shards(n_grp, n_blk, features, col_scale, row_scale, tiles, tile_cols, weight, cotangent, train_mask):
    nodes, fin = features.shape
    hid_width = weight.shape[1]
    tile = tiles.shape[1]
    n = n_grp * n_blk
    pieces = n * 8 * 128 == fin * hid_width
    any_space = pl.BlockSpec(memory_space=pl.ANY)
    vmem = pl.BlockSpec(memory_space=pltpu.VMEM)
    if pieces:
        grad_scratch = [
            pltpu.VMEM((n, 8, 128), GRAD_LINK),
            pltpu.VMEM((n - 1, 8, 128), GRAD_LINK),
            pltpu.VMEM((n, 8, 128), GRAD_LINK),
        ]
    else:
        grad_scratch = [
            pltpu.VMEM((8, 128), F32),
            pltpu.VMEM((8, 128), F32),
            pltpu.VMEM((fin, hid_width), F32),
        ]
    dma = pltpu.SemaphoreType.DMA
    hidden, grad = pl.pallas_call(
        functools.partial(kernel, n_grp, n_blk, pieces),
        out_shape=(jax.ShapeDtypeStruct((nodes, hid_width), BF16),
                   jax.ShapeDtypeStruct((fin, hid_width), F32)),
        in_specs=[pl.BlockSpec(memory_space=pltpu.SMEM)] + [any_space] * 7,
        out_specs=(any_space, vmem if pieces else any_space),
        scratch_shapes=[
            pltpu.VMEM((nodes, fin), BF16),
            pltpu.VMEM((1, nodes), F32),
            pltpu.VMEM((1, nodes), F32),
            pltpu.VMEM((1, nodes), jnp.int32),
            pltpu.VMEM((fin, hid_width), BF16),
            pltpu.VMEM((nodes, hid_width), BF16),
            pltpu.VMEM(tiles.shape, BF16),
            pltpu.VMEM((n_grp, tile, fin), BF16),
            pltpu.VMEM((tile, fin), F32),
            pltpu.VMEM((n_blk - 1, tile, fin), BF16),
            pltpu.VMEM((n_blk - 1, tile, fin), BF16),
            pltpu.VMEM((nodes, hid_width), BF16),
            *grad_scratch,
            dma((6,)), dma((n_blk,)), dma((n_grp - 1,)), dma((n_grp - 1,)),
            dma((n_blk - 1,)), dma((n_blk - 1,)), dma((4,)), dma((2,)),
        ],
        compiler_params=pltpu.CompilerParams(
            collective_id=0, has_side_effects=True, vmem_limit_bytes=48 * 1024 * 1024),
    )(tile_cols, features, col_scale.reshape(1, nodes), row_scale.reshape(1, nodes), tiles, weight,
      cotangent, train_mask.reshape(1, nodes))
    if not pieces:
        grad = lax.psum(grad, ("grp", "blk"))
    return hidden, grad


def solution(mesh):
    in_specs = (
        P(("grp", "blk"), None),
        P(("grp", "blk")),
        P(("grp", "blk")),
        P(("grp", "blk"), None, None),
        P(("grp", "blk")),
        P(),
        P(("grp", "blk"), None),
        P(("grp", "blk")),
    )
    out_specs = (P(("grp", "blk"), None), P())
    body = functools.partial(shards, mesh.shape["grp"], mesh.shape["blk"])
    return jax.shard_map(body, mesh=mesh, in_specs=in_specs, out_specs=out_specs, check_vma=False)
```

time: 209 us -> 35 us (0.17)
  waiting for transfers between devices: 167 us -> 0 us
  Pallas kernels: 0 us -> 28.4 us
  blocking collectives: 13.5 us -> 0 us
  between operations: 14.1 us -> 0.68 us
  starting transfers between devices: 3.64 us -> 0 us
  matrix products: 2.43 us -> 0 us
    psum x1 -> x0, waiting for transfers between devices: 122 us -> none  [shards(): weight_grad = lax.psum(local_grad, ('grp', 'blk'))]
    all_gather x1 -> x0, waiting for transfers between devices: 45.2 us -> none  [shards(): everything = lax.all_gather(scaled, ('grp', 'blk'), axis=0, tiled=True)]
    pallas_call x0 -> x1, Pallas kernels: none -> 28.4 us  [shards(): pl.pallas_call(functools.partial(kernel, n_grp, n_blk, pieces), out_shape...]
    all_to_all x1 -> x0, blocking collectives: 13.5 us -> none  [shards(): lax.all_to_all(tile_cols, 'blk', split_axis=0, concat_axis=0, tiled=True)]
    all_to_all x1 -> x0, starting transfers between devices: 3.56 us -> none  [shards(): lax.all_to_all(tiles, 'blk', split_axis=0, concat_axis=0, tiled=True)]
    gather x2 -> x0, local copies, waits for them, and re-layouts: 2.64 us -> none  [shards(): picked = jnp.take(everything, global_cols.reshape(-1), axis=0)]
    dot_general x3 -> x0, matrix products: 2.43 us -> none  [the longest x1 1.04 us: shards(): local_grad = jnp.dot(mixed.T, delta, precision=lax.Precision.HIGHEST)]
    unnamed x11 -> x18, local copies, waits for them, and re-layouts: 3.43 us -> 5.62 us
  transfers between devices with their start and end apart: 3 -> 0, of which waited for: 2 -> 0; matrix products, arithmetic and copies ran while one was open for 1% -> 0% of each run, Pallas kernels for 0% -> 0%
where the time goes in v1:
time: 35 us; the launch traced here: 34.7 us
  Pallas kernels  28.4 us (81%)
  local copies, waits for them, and re-layouts  5.62 us (16%)
  between operations  0.68 us (2%)
    pallas_call x1, Pallas kernels, shards(): pl.pallas_call(functools.partial(kernel, n_grp, n_blk, pieces), out_shape...  28.4 us
    unnamed x18, local copies, waits for them, and re-layouts  5.62 us

profile of v1, /device:TPU:0, one launch (start us, length us, event | category | flops | bytes accessed | tf_op | source)
XLA Modules:
  0.0 34.7 jit_solution(7113887772672236787)
XLA Ops:
  0.6 0.0 copy-start.7
  0.6 0.0 copy-start.4
  0.7 0.0 copy-start.5
  0.7 0.0 copy-start.6
  0.7 0.6 %copy-done.7 = s32[128]{0:T(128)S(1)} copy-done((s32[128]{0:T(128)S(1)}, s32[128]{0:T(128)}, u32[]{:S(2)}) %copy-start.7) | copy-done | bytes 536
  1.3 0.0 copy-done.4
  1.3 0.0 copy-done.5
  1.3 0.0 copy-done.6
  1.3 0.0 copy-start
  1.3 1.2 %copy-done = bf16[32,128,128]{2,1,0:T(8,128)(2,1)S(1)} copy-done((bf16[32,128,128]{2,1,0:T(8,128)(2,1)S(1)}, bf16[32,128,128]{2,1,0:T(8,128)(2,1)}, u32[]{:S(2)}) %copy-start) | copy-done | bytes 1048600
  2.6 0.0 copy-start.1
  2.6 0.8 %copy-done.1 = bf16[128,256]{1,0:T(8,128)(2,1)S(1)} copy-done((bf16[128,256]{1,0:T(8,128)(2,1)S(1)}, bf16[128,256]{1,0:T(8,128)(2,1)}, u32[]{:S(2)}) %copy-start.1) | copy-done | bytes 65560
  3.4 0.0 copy-start.2
  3.4 0.8 %copy-done.2 = bf16[128,256]{1,0:T(8,128)(2,1)S(1)} copy-done((bf16[128,256]{1,0:T(8,128)(2,1)S(1)}, bf16[128,256]{1,0:T(8,128)(2,1)}, u32[]{:S(2)}) %copy-start.2) | copy-done | bytes 65560
  4.2 0.0 copy-start.3
  4.2 0.8 %copy-done.3 = bf16[128,128]{1,0:T(8,128)(2,1)S(1)} copy-done((bf16[128,128]{1,0:T(8,128)(2,1)S(1)}, bf16[128,128]{1,0:T(8,128)(2,1)}, u32[]{:S(2)}) %copy-start.3) | copy-done | bytes 32792
  5.0 28.4 %shard_map.95 = (bf16[128,256]{1,0:T(8,128)(2,1)S(1)}, f32[128,256]{1,0:T(8,128)S(1)}) custom-call(s32[32]{0:T(128)S(1)} %copy-done.4, bf16[128,128]{1,0:T(8,128)(2,1)S(1)} %copy-done.3, f32[1,128]{1,0:T(1,128)S(1)} %bitcast.3, f32[1,128]{1,0:T(1,128)S(1)} %bitcast.4, bf16[32,128,128]{2,1,0:T(8,128)(2,1)S(1)} %copy-done, bf16[128,256]{1,0:T(8,128)(2,1)S(1)} %copy-done.1, ...), custom_call_target="tpu_custom_call" | custom-call | tf_op jit(solution)/shard_map/pallas_call | solution.py:200
  33.4 0.6 %copy.12 = bf16[128,256]{1,0:T(8,128)(2,1)} copy(bf16[128,256]{1,0:T(8,128)(2,1)S(1)} %get-tuple-element.4) | data formatting | bytes 131072
  34.1 0.7 %copy.13 = f32[128,256]{1,0:T(8,128)} copy(f32[128,256]{1,0:T(8,128)S(1)} %get-tuple-element.5) | data formatting | bytes 262144
Async XLA Ops:
  0.6 0.7 %copy-start.7 = (s32[128]{0:T(128)S(1)}, s32[128]{0:T(128)}, u32[]{:S(2)}) copy-start(s32[128]{0:T(128)} %param.15) | copy-start | bytes 1540
  0.6 0.7 %copy-start.4 = (s32[32]{0:T(128)S(1)}, s32[32]{0:T(128)}, u32[]{:S(2)}) copy-start(s32[32]{0:T(128)} %cols.1) | copy-start | bytes 388
  0.7 0.7 %copy-start.5 = (f32[128]{0:T(128)S(1)}, f32[128]{0:T(128)}, u32[]{:S(2)}) copy-start(f32[128]{0:T(128)} %param.9) | copy-start | bytes 1540
  0.7 0.7 %copy-start.6 = (f32[128]{0:T(128)S(1)}, f32[128]{0:T(128)}, u32[]{:S(2)}) copy-start(f32[128]{0:T(128)} %param.10) | copy-start | bytes 1540
  1.3 1.2 %copy-start = (bf16[32,128,128]{2,1,0:T(8,128)(2,1)S(1)}, bf16[32,128,128]{2,1,0:T(8,128)(2,1)}, u32[]{:S(2)}) copy-start(bf16[32,128,128]{2,1,0:T(8,128)(2,1)} %tiles.1) | copy-start | bytes 3145732
  2.6 0.8 %copy-start.1 = (bf16[128,256]{1,0:T(8,128)(2,1)S(1)}, bf16[128,256]{1,0:T(8,128)(2,1)}, u32[]{:S(2)}) copy-start(bf16[128,256]{1,0:T(8,128)(2,1)} %weight.1) | copy-start | bytes 196612
  3.4 0.8 %copy-start.2 = (bf16[128,256]{1,0:T(8,128)(2,1)S(1)}, bf16[128,256]{1,0:T(8,128)(2,1)}, u32[]{:S(2)}) copy-start(bf16[128,256]{1,0:T(8,128)(2,1)} %cotangent.1) | copy-start | bytes 196612
  4.2 0.8 %copy-start.3 = (bf16[128,128]{1,0:T(8,128)(2,1)S(1)}, bf16[128,128]{1,0:T(8,128)(2,1)}, u32[]{:S(2)}) copy-start(bf16[128,128]{1,0:T(8,128)(2,1)} %features.1) | copy-start | bytes 98308

commit v2 on v1

--- a/solution.py
+++ b/solution.py
@@ -15,6 +15,7 @@
 F32 = jnp.float32
 BF16 = jnp.bfloat16
 GRAD_LINK = F32
+VLIM = 64 * 1024 * 1024
 
 
 def far_first(count):
@@ -30,10 +31,26 @@
     return jnp.broadcast_to(row, (width, row.shape[1])).T
 
 
-def kernel(n_grp, n_blk, pieces, cols, features, col_scale, row_scale, tiles, weight, cotangent,
-           train_mask, hidden_out, grad_out, feat, cscale, rscale, mask, wgt, cot, held, sources,
-           mine, outgoing, arrived, hid, grad_parts, grad_in, grad_all, in_sems, tile_sems, src_send,
-           src_recv, part_send, part_recv, grad_sems, out_sems):
+def finish(pieces, hid, grad, hidden_out, grad_out, flat, sems):
+    first = pltpu.make_async_copy(hid, hidden_out, sems.at[0])
+    first.start()
+    if pieces:
+        wide = flat.shape[1] // 128
+        for piece in range(grad.shape[0]):
+            at, lane = piece // wide * 8, piece % wide * 128
+            flat[at:at + 8, lane:lane + 128] = grad[piece].astype(F32)
+    else:
+        flat[...] = grad[...]
+    second = pltpu.make_async_copy(flat, grad_out, sems.at[1])
+    second.start()
+    first.wait()
+    second.wait()
+
+
+def kernel(n_grp, n_blk, pieces, cols_in, features, col_scale, row_scale, tiles, weight, cotangent,
+           train_mask, hid, grad_all, cols, feat, cscale, rscale, mask, wgt, cot, held, sources,
+           mine, outgoing, arrived, grad_parts, grad_in, in_sems, tile_sems, src_send,
+           src_recv, part_send, part_recv, grad_sems):
     g, b = lax.axis_index("grp"), lax.axis_index("blk")
     order = far_first(n_blk) + [0]
 
@@ -49,6 +66,8 @@
         return copy
 
     first = [load(features, feat, in_sems.at[0]), load(col_scale, cscale, in_sems.at[1])]
+
+    cols_load = load(cols_in, cols, in_sems.at[6])
 
     barrier = pltpu.get_barrier_semaphore()
     for step in range(1, n_grp):
@@ -80,6 +99,7 @@
             device_id=(grp_peer(step), b), device_id_type=MESH)
         copy.start()
         src_copies.append(copy)
+    cols_load.wait()
     for copy in tile_loads:
         copy.wait()
     for copy in src_copies:
@@ -123,7 +143,6 @@
     bent = jnp.tanh(ROOT * pre * (1.0 + CUBE * square))
     half = 0.5 * (1.0 + bent)
     hid[...] = (pre * half).astype(BF16)
-    out_copy = load(hid, hidden_out, out_sems.at[0])
     slope = half + 0.5 * pre * (1.0 - bent * bent) * (ROOT * (1.0 + 3.0 * CUBE * square))
     delta = slope * masked
 
@@ -133,8 +152,6 @@
                    jnp.concatenate([d_high, d_high, d_low], axis=0), preferred_element_type=F32)
     if not pieces:
         grad_all[...] = grad
-        load(grad_all, grad_out, out_sems.at[1]).wait()
-        out_copy.wait()
         return
 
     n = n_grp * n_blk
@@ -170,10 +187,6 @@
     pltpu.make_async_copy(some, some, grad_sems.at[0]).wait()
     pltpu.make_async_copy(some, some, grad_sems.at[2]).wait()
     pltpu.make_async_copy(some, some, grad_sems.at[3]).wait()
-    for piece in range(n):
-        at, lane = piece // wide * 8, piece % wide * 128
-        grad_out[at:at + 8, lane:lane + 128] = grad_all[piece].astype(F32)
-    out_copy.wait()
 
 
 def shards(n_grp, n_blk, features, col_scale, row_scale, tiles, tile_cols, weight, cotangent, train_mask):
@@ -182,28 +195,23 @@
     tile = tiles.shape[1]
     n = n_grp * n_blk
     pieces = n * 8 * 128 == fin * hid_width
-    any_space = pl.BlockSpec(memory_space=pl.ANY)
+    hbm = pl.BlockSpec(memory_space=pltpu.HBM)
     vmem = pl.BlockSpec(memory_space=pltpu.VMEM)
     if pieces:
-        grad_scratch = [
-            pltpu.VMEM((n, 8, 128), GRAD_LINK),
-            pltpu.VMEM((n - 1, 8, 128), GRAD_LINK),
-            pltpu.VMEM((n, 8, 128), GRAD_LINK),
-        ]
+        grad_scratch = [pltpu.VMEM((n, 8, 128), GRAD_LINK), pltpu.VMEM((n - 1, 8, 128), GRAD_LINK)]
+        grad_shape = jax.ShapeDtypeStruct((n, 8, 128), GRAD_LINK)
     else:
-        grad_scratch = [
-            pltpu.VMEM((8, 128), F32),
-            pltpu.VMEM((8, 128), F32),
-            pltpu.VMEM((fin, hid_width), F32),
-        ]
+        grad_scratch = [pltpu.VMEM((8, 128), F32), pltpu.VMEM((8, 128), F32)]
+        grad_shape = jax.ShapeDtypeStruct((fin, hid_width), F32)
     dma = pltpu.SemaphoreType.DMA
+    hidden_shape = jax.ShapeDtypeStruct((nodes, hid_width), BF16)
     hidden, grad = pl.pallas_call(
         functools.partial(kernel, n_grp, n_blk, pieces),
-        out_shape=(jax.ShapeDtypeStruct((nodes, hid_width), BF16),
-                   jax.ShapeDtypeStruct((fin, hid_width), F32)),
-        in_specs=[pl.BlockSpec(memory_space=pltpu.SMEM)] + [any_space] * 7,
-        out_specs=(any_space, vmem if pieces else any_space),
+        out_shape=(hidden_shape, grad_shape),
+        in_specs=[hbm] * 8,
+        out_specs=(vmem, vmem),
         scratch_shapes=[
+            pltpu.SMEM(tile_cols.shape, jnp.int32),
             pltpu.VMEM((nodes, fin), BF16),
             pltpu.VMEM((1, nodes), F32),
             pltpu.VMEM((1, nodes), F32),
@@ -215,15 +223,22 @@
             pltpu.VMEM((tile, fin), F32),
             pltpu.VMEM((n_blk - 1, tile, fin), BF16),
             pltpu.VMEM((n_blk - 1, tile, fin), BF16),
-            pltpu.VMEM((nodes, hid_width), BF16),
             *grad_scratch,
-            dma((6,)), dma((n_blk,)), dma((n_grp - 1,)), dma((n_grp - 1,)),
-            dma((n_blk - 1,)), dma((n_blk - 1,)), dma((4,)), dma((2,)),
+            dma((7,)), dma((n_blk,)), dma((n_grp - 1,)), dma((n_grp - 1,)),
+            dma((n_blk - 1,)), dma((n_blk - 1,)), dma((4,)),
         ],
         compiler_params=pltpu.CompilerParams(
-            collective_id=0, has_side_effects=True, vmem_limit_bytes=48 * 1024 * 1024),
+            collective_id=0, has_side_effects=True, vmem_limit_bytes=VLIM),
     )(tile_cols, features, col_scale.reshape(1, nodes), row_scale.reshape(1, nodes), tiles, weight,
       cotangent, train_mask.reshape(1, nodes))
+    hidden, grad = pl.pallas_call(
+        functools.partial(finish, pieces),
+        out_shape=(hidden_shape, jax.ShapeDtypeStruct((fin, hid_width), F32)),
+        in_specs=[vmem, vmem],
+        out_specs=(hbm, hbm),
+        scratch_shapes=[pltpu.VMEM((fin, hid_width), F32), dma((2,))],
+        compiler_params=pltpu.CompilerParams(vmem_limit_bytes=1024 * 1024),
+    )(hidden, grad)
     if not pieces:
         grad = lax.psum(grad, ("grp", "blk"))
     return hidden, grad

time: 35 us -> 31.8 us (0.909)
  local copies, waits for them, and re-layouts: 5.62 us -> 1.74 us
  Pallas kernels: 28.4 us -> 29.3 us
    unnamed x18 -> x4, local copies, waits for them, and re-layouts: 5.62 us -> 1.74 us
    pallas_call x0 -> x1, Pallas kernels: none -> 0.69 us  [shards(): pl.pallas_call(functools.partial(finish, pieces), out_shape=(hidden_shape...]
where the time goes in v2:
time: 31.8 us; the launch traced here: 31.6 us
  Pallas kernels  29.3 us (92%)
  local copies, waits for them, and re-layouts  1.74 us (5%)
  between operations  0.65 us (2%)
    pallas_call x1, Pallas kernels, shards(): pl.pallas_call(functools.partial(kernel, n_grp, n_blk, pieces), out_shape...  28.6 us
    unnamed x4, local copies, waits for them, and re-layouts  1.74 us
    pallas_call x1, Pallas kernels, shards(): pl.pallas_call(functools.partial(finish, pieces), out_shape=(hidden_shape...  0.69 us

profile of v2, /device:TPU:0, one launch (start us, length us, event | category | flops | bytes accessed | tf_op | source)
XLA Modules:
  0.0 31.6 jit_solution(7010803862757864932)
XLA Ops:
  0.6 28.6 %shard_map.95 = (bf16[128,256]{1,0:T(8,128)(2,1)}, f32[32,8,128]{2,1,0:T(8,128)}) custom-call(s32[32]{0:T(128)} %cols_in.1, bf16[128,128]{1,0:T(8,128)(2,1)} %features.1, f32[1,128]{1,0:T(1,128)} %bitcast.3, f32[1,128]{1,0:T(1,128)} %bitcast.4, bf16[32,128,128]{2,1,0:T(8,128)(2,1)} %tiles.1, bf16[128,256]{1,0:T(8,128)(2,1)} %weight.1, ...), custom_call_target="tpu_custom_call" | custom-call | tf_op jit(solution)/shard_map/pallas_call | solution.py:208
  29.2 0.0 copy-start
  29.2 0.9 %copy-done = f32[32,8,128]{2,1,0:T(8,128)S(1)} copy-done((f32[32,8,128]{2,1,0:T(8,128)S(1)}, f32[32,8,128]{2,1,0:T(8,128)}, u32[]{:S(2)}) %copy-start) | copy-done | bytes 131096
  30.1 0.0 copy-start.1
  30.1 0.8 %copy-done.1 = bf16[128,256]{1,0:T(8,128)(2,1)S(1)} copy-done((bf16[128,256]{1,0:T(8,128)(2,1)S(1)}, bf16[128,256]{1,0:T(8,128)(2,1)}, u32[]{:S(2)}) %copy-start.1) | copy-done | bytes 65560
  30.9 0.7 %shard_map.96 = (bf16[128,256]{1,0:T(8,128)(2,1)}, f32[128,256]{1,0:T(8,128)}) custom-call(bf16[128,256]{1,0:T(8,128)(2,1)S(1)} %copy-done.1, f32[32,8,128]{2,1,0:T(8,128)S(1)} %copy-done), custom_call_target="tpu_custom_call" | custom-call | tf_op jit(solution)/shard_map/pallas_call | solution.py:234
Async XLA Ops:
  29.2 0.9 %copy-start = (f32[32,8,128]{2,1,0:T(8,128)S(1)}, f32[32,8,128]{2,1,0:T(8,128)}, u32[]{:S(2)}) copy-start(f32[32,8,128]{2,1,0:T(8,128)} %get-tuple-element.5.grad) | copy-start | bytes 393220
  30.1 0.8 %copy-start.1 = (bf16[128,256]{1,0:T(8,128)(2,1)S(1)}, bf16[128,256]{1,0:T(8,128)(2,1)}, u32[]{:S(2)}) copy-start(bf16[128,256]{1,0:T(8,128)(2,1)} %get-tuple-element.4.hid) | copy-start | bytes 196612

commit v3 on v2

--- a/solution.py
+++ b/solution.py
@@ -14,7 +14,7 @@
 MESH = pl.DeviceIdType.MESH
 F32 = jnp.float32
 BF16 = jnp.bfloat16
-GRAD_LINK = F32
+GRAD_LINK = BF16
 VLIM = 64 * 1024 * 1024
 
 
@@ -31,26 +31,10 @@
     return jnp.broadcast_to(row, (width, row.shape[1])).T
 
 
-def finish(pieces, hid, grad, hidden_out, grad_out, flat, sems):
-    first = pltpu.make_async_copy(hid, hidden_out, sems.at[0])
-    first.start()
-    if pieces:
-        wide = flat.shape[1] // 128
-        for piece in range(grad.shape[0]):
-            at, lane = piece // wide * 8, piece % wide * 128
-            flat[at:at + 8, lane:lane + 128] = grad[piece].astype(F32)
-    else:
-        flat[...] = grad[...]
-    second = pltpu.make_async_copy(flat, grad_out, sems.at[1])
-    second.start()
-    first.wait()
-    second.wait()
-
-
 def kernel(n_grp, n_blk, pieces, cols_in, features, col_scale, row_scale, tiles, weight, cotangent,
-           train_mask, hid, grad_all, cols, feat, cscale, rscale, mask, wgt, cot, held, sources,
-           mine, outgoing, arrived, grad_parts, grad_in, in_sems, tile_sems, src_send,
-           src_recv, part_send, part_recv, grad_sems):
+           train_mask, hidden_out, grad_out, cols, feat, cscale, rscale, mask, wgt, cot, held, sources,
+           mine, outgoing, arrived, hid, flat, grad_all, grad_parts, grad_in, in_sems, tile_sems, src_send,
+           src_recv, part_send, part_recv, grad_sems, out_sems):
     g, b = lax.axis_index("grp"), lax.axis_index("blk")
     order = far_first(n_blk) + [0]
 
@@ -142,7 +126,8 @@
     square = pre * pre
     bent = jnp.tanh(ROOT * pre * (1.0 + CUBE * square))
     half = 0.5 * (1.0 + bent)
-    hid[...] = (pre * half).astype(BF16)
+    hid[...] = pre * half
+    hidden_copy = load(hid, hidden_out, out_sems.at[0])
     slope = half + 0.5 * pre * (1.0 - bent * bent) * (ROOT * (1.0 + 3.0 * CUBE * square))
     delta = slope * masked
 
@@ -151,42 +136,64 @@
     grad = jnp.dot(jnp.concatenate([high_t, low_t, high_t], axis=1),
                    jnp.concatenate([d_high, d_high, d_low], axis=0), preferred_element_type=F32)
     if not pieces:
-        grad_all[...] = grad
+        flat[...] = grad
+        load(flat, grad_out, out_sems.at[1]).wait()
+        hidden_copy.wait()
         return
 
     n = n_grp * n_blk
     me = g * n_blk + b
-    wide = grad.shape[1] // 128
-    for piece in range(n):
-        at, lane = piece // wide * 8, piece % wide * 128
-        grad_parts[piece] = grad[at:at + 8, lane:lane + 128].astype(GRAD_LINK)
+    span, first_blk = n_blk // 2, n_blk // 4
+    owners = n_grp * span
+    owner = (b >= first_blk) & (b < first_blk + span)
+    seat = g * span + (b - first_blk)
+    for piece in range(owners):
+        grad_parts[piece] = grad[piece * 8:piece * 8 + 8].astype(GRAD_LINK)
 
     def scatter(step, _):
-        to = lax.rem(me + step, n)
-        pltpu.make_async_remote_copy(
-            src_ref=grad_parts.at[to], dst_ref=grad_in.at[n - 1 - step],
-            send_sem=grad_sems.at[0], recv_sem=grad_sems.at[1],
-            device_id=(to // n_blk, lax.rem(to, n_blk)), device_id_type=MESH).start()
+        to = lax.rem(me + step, owners)
+        to_g, to_b = to // span, first_blk + lax.rem(to, span)
+
+        @pl.when(to_g * n_blk + to_b != me)
+        def _():
+            pltpu.make_async_remote_copy(
+                src_ref=grad_parts.at[to], dst_ref=grad_in.at[me],
+                send_sem=grad_sems.at[0], recv_sem=grad_sems.at[1],
+                device_id=(to_g, to_b), device_id_type=MESH).start()
         return 0
 
-    lax.fori_loop(1, n, scatter, 0)
-    some = grad_parts.at[pl.ds(0, n - 1)]
-    pltpu.make_async_copy(grad_in, grad_in, grad_sems.at[1]).wait()
-    summed = grad_parts[me].astype(F32) + jnp.sum(grad_in[...].astype(F32), axis=0)
-    grad_all[me] = summed.astype(GRAD_LINK)
-
-    def gather(step, _):
-        to = lax.rem(me + step, n)
-        pltpu.make_async_remote_copy(
-            src_ref=grad_all.at[me], dst_ref=grad_all.at[me],
-            send_sem=grad_sems.at[2], recv_sem=grad_sems.at[3],
-            device_id=(to // n_blk, lax.rem(to, n_blk)), device_id_type=MESH).start()
-        return 0
-
-    lax.fori_loop(1, n, gather, 0)
-    pltpu.make_async_copy(some, some, grad_sems.at[0]).wait()
-    pltpu.make_async_copy(some, some, grad_sems.at[2]).wait()
-    pltpu.make_async_copy(some, some, grad_sems.at[3]).wait()
+    lax.fori_loop(0, owners, scatter, 0)
+    some = grad_parts.at[pl.ds(0, owners - 1)]
+
+    @pl.when(owner)
+    def _():
+        grad_in[me] = grad_parts[seat]
+        others = grad_in.at[pl.ds(0, n - 1)]
+        pltpu.make_async_copy(others, others, grad_sems.at[1]).wait()
+        grad_all[seat] = jnp.sum(grad_in[...].astype(F32), axis=0).astype(GRAD_LINK)
+
+        def gather(step, _):
+            to = lax.rem(me + step, n)
+            pltpu.make_async_remote_copy(
+                src_ref=grad_all.at[seat], dst_ref=grad_all.at[seat],
+                send_sem=grad_sems.at[2], recv_sem=grad_sems.at[3],
+                device_id=(to // n_blk, lax.rem(to, n_blk)), device_id_type=MESH).start()
+            return 0
+
+        lax.fori_loop(1, n, gather, 0)
+        pltpu.make_async_copy(some, some, grad_sems.at[0]).wait()
+        pltpu.make_async_copy(some, some, grad_sems.at[3]).wait()
+        pltpu.make_async_copy(others, others, grad_sems.at[2]).wait()
+
+    @pl.when(jnp.logical_not(owner))
+    def _():
+        pltpu.make_async_copy(grad_parts, grad_parts, grad_sems.at[0]).wait()
+        pltpu.make_async_copy(grad_parts, grad_parts, grad_sems.at[3]).wait()
+
+    for piece in range(owners):
+        flat[piece * 8:piece * 8 + 8] = grad_all[piece]
+    load(flat, grad_out, out_sems.at[1]).wait()
+    hidden_copy.wait()
 
 
 def shards(n_grp, n_blk, features, col_scale, row_scale, tiles, tile_cols, weight, cotangent, train_mask):
@@ -194,22 +201,21 @@
     hid_width = weight.shape[1]
     tile = tiles.shape[1]
     n = n_grp * n_blk
-    pieces = n * 8 * 128 == fin * hid_width
+    pieces = n_grp * (n_blk // 2) * 8 == fin
     hbm = pl.BlockSpec(memory_space=pltpu.HBM)
-    vmem = pl.BlockSpec(memory_space=pltpu.VMEM)
     if pieces:
-        grad_scratch = [pltpu.VMEM((n, 8, 128), GRAD_LINK), pltpu.VMEM((n - 1, 8, 128), GRAD_LINK)]
-        grad_shape = jax.ShapeDtypeStruct((n, 8, 128), GRAD_LINK)
+        spare, landing = (fin // 8, 8, hid_width), (n, 8, hid_width)
     else:
-        grad_scratch = [pltpu.VMEM((8, 128), F32), pltpu.VMEM((8, 128), F32)]
-        grad_shape = jax.ShapeDtypeStruct((fin, hid_width), F32)
+        spare = landing = (1, 8, 128)
+    grad_type = GRAD_LINK if pieces else F32
+    grad_shape = jax.ShapeDtypeStruct((fin, hid_width), grad_type)
     dma = pltpu.SemaphoreType.DMA
-    hidden_shape = jax.ShapeDtypeStruct((nodes, hid_width), BF16)
+    hidden_shape = jax.ShapeDtypeStruct((nodes, hid_width), F32)
     hidden, grad = pl.pallas_call(
         functools.partial(kernel, n_grp, n_blk, pieces),
         out_shape=(hidden_shape, grad_shape),
         in_specs=[hbm] * 8,
-        out_specs=(vmem, vmem),
+        out_specs=(hbm, hbm),
         scratch_shapes=[
             pltpu.SMEM(tile_cols.shape, jnp.int32),
             pltpu.VMEM((nodes, fin), BF16),
@@ -223,25 +229,21 @@
             pltpu.VMEM((tile, fin), F32),
             pltpu.VMEM((n_blk - 1, tile, fin), BF16),
             pltpu.VMEM((n_blk - 1, tile, fin), BF16),
-            *grad_scratch,
+            pltpu.VMEM((nodes, hid_width), F32),
+            pltpu.VMEM((fin, hid_width), grad_type),
+            pltpu.VMEM(spare, GRAD_LINK),
+            pltpu.VMEM(spare, GRAD_LINK),
+            pltpu.VMEM(landing, GRAD_LINK),
             dma((7,)), dma((n_blk,)), dma((n_grp - 1,)), dma((n_grp - 1,)),
-            dma((n_blk - 1,)), dma((n_blk - 1,)), dma((4,)),
+            dma((n_blk - 1,)), dma((n_blk - 1,)), dma((4,)), dma((2,)),
         ],
         compiler_params=pltpu.CompilerParams(
             collective_id=0, has_side_effects=True, vmem_limit_bytes=VLIM),
     )(tile_cols, features, col_scale.reshape(1, nodes), row_scale.reshape(1, nodes), tiles, weight,
       cotangent, train_mask.reshape(1, nodes))
-    hidden, grad = pl.pallas_call(
-        functools.partial(finish, pieces),
-        out_shape=(hidden_shape, jax.ShapeDtypeStruct((fin, hid_width), F32)),
-        in_specs=[vmem, vmem],
-        out_specs=(hbm, hbm),
-        scratch_shapes=[pltpu.VMEM((fin, hid_width), F32), dma((2,))],
-        compiler_params=pltpu.CompilerParams(vmem_limit_bytes=1024 * 1024),
-    )(hidden, grad)
     if not pieces:
         grad = lax.psum(grad, ("grp", "blk"))
-    return hidden, grad
+    return hidden.astype(BF16), grad.astype(F32)
 
 
 def solution(mesh):

time: 31.8 us -> 29.5 us (0.928)
  Pallas kernels: 29.3 us -> 26.5 us
  other arithmetic: 0 us -> 2.24 us
  local copies, waits for them, and re-layouts: 1.74 us -> 0.01 us
    convert_element_type x0 -> x2, other arithmetic: none -> 2.24 us  [shards(): return (hidden.astype(BF16), grad.astype(F32))]
    pallas_call x1, Pallas kernels: 28.6 us -> 26.5 us  [shards(): pl.pallas_call(functools.partial(kernel, n_grp, n_blk, pieces), out_shape...]
    unnamed x4 -> x2, local copies, waits for them, and re-layouts: 1.74 us -> 0.01 us
    pallas_call x1 -> x0, Pallas kernels: 0.69 us -> none  [shards(): pl.pallas_call(functools.partial(finish, pieces), out_shape=(hidden_shape...]
where the time goes in v3:
time: 29.5 us; the launch traced here: 29.4 us
  Pallas kernels  26.5 us (90%)
  other arithmetic  2.24 us (8%)
  between operations  0.65 us (2%)
    pallas_call x1, Pallas kernels, shards(): pl.pallas_call(functools.partial(kernel, n_grp, n_blk, pieces), out_shape...  26.5 us
    convert_element_type x2, other arithmetic, shards(): return (hidden.astype(BF16), grad.astype(F32))  2.24 us

profile of v3, /device:TPU:0, one launch (start us, length us, event | category | flops | bytes accessed | tf_op | source)
XLA Modules:
  0.0 29.4 jit_solution(9532869396563633694)
XLA Ops:
  0.6 26.5 %shard_map.95 = (f32[128,256]{1,0:T(8,128)}, bf16[128,256]{1,0:T(8,128)(2,1)}) custom-call(s32[32]{0:T(128)} %cols_in.1, bf16[128,128]{1,0:T(8,128)(2,1)} %features.1, f32[1,128]{1,0:T(1,128)} %bitcast.3, f32[1,128]{1,0:T(1,128)} %bitcast.4, bf16[32,128,128]{2,1,0:T(8,128)(2,1)} %tiles.1, bf16[128,256]{1,0:T(8,128)(2,1)} %weight.1, ...), custom_call_target="tpu_custom_call" | custom-call | tf_op jit(solution)/shard_map/pallas_call | solution.py:214
  27.1 0.0 copy-start
  27.1 1.6 %convert_element_type.6 = bf16[128,256]{1,0:T(8,128)(2,1)} convert(f32[128,256]{1,0:T(8,128)} %get-tuple-element.4) | non-fusion elementwise | flops 32768 | bytes 196608 | tf_op jit(solution)/shard_map/convert_element_type | solution.py:246
  28.7 0.0 copy-done
  28.7 0.7 %convert_element_type.7 = f32[128,256]{1,0:T(8,128)} convert(bf16[128,256]{1,0:T(8,128)(2,1)S(1)} %copy-done) | non-fusion elementwise | flops 32768 | bytes 196608 | tf_op jit(solution)/shard_map/convert_element_type | solution.py:246
Async XLA Ops:
  27.1 1.6 %copy-start = (bf16[128,256]{1,0:T(8,128)(2,1)S(1)}, bf16[128,256]{1,0:T(8,128)(2,1)}, u32[]{:S(2)}) copy-start(bf16[128,256]{1,0:T(8,128)(2,1)} %get-tuple-element.5) | copy-start | bytes 196612

commit v4 on v3

--- a/solution.py
+++ b/solution.py
@@ -32,7 +32,7 @@
 
 
 def kernel(n_grp, n_blk, pieces, cols_in, features, col_scale, row_scale, tiles, weight, cotangent,
-           train_mask, hidden_out, grad_out, cols, feat, cscale, rscale, mask, wgt, cot, held, sources,
+           train_mask, packed, cols, feat, cscale, rscale, mask, wgt, cot, held, sources,
            mine, outgoing, arrived, hid, flat, grad_all, grad_parts, grad_in, in_sems, tile_sems, src_send,
            src_recv, part_send, part_recv, grad_sems, out_sems):
     g, b = lax.axis_index("grp"), lax.axis_index("blk")
@@ -126,8 +126,8 @@
     square = pre * pre
     bent = jnp.tanh(ROOT * pre * (1.0 + CUBE * square))
     half = 0.5 * (1.0 + bent)
-    hid[...] = pre * half
-    hidden_copy = load(hid, hidden_out, out_sems.at[0])
+    hid[...] = (pre * half).astype(hid.dtype)
+    hidden_copy = load(hid, packed.at[pl.ds(0, hid.shape[0])], out_sems.at[0])
     slope = half + 0.5 * pre * (1.0 - bent * bent) * (ROOT * (1.0 + 3.0 * CUBE * square))
     delta = slope * masked
 
@@ -137,7 +137,7 @@
                    jnp.concatenate([d_high, d_high, d_low], axis=0), preferred_element_type=F32)
     if not pieces:
         flat[...] = grad
-        load(flat, grad_out, out_sems.at[1]).wait()
+        load(flat, packed.at[pl.ds(hid.shape[0], flat.shape[0])], out_sems.at[1]).wait()
         hidden_copy.wait()
         return
 
@@ -192,7 +192,7 @@
 
     for piece in range(owners):
         flat[piece * 8:piece * 8 + 8] = grad_all[piece]
-    load(flat, grad_out, out_sems.at[1]).wait()
+    load(flat, packed.at[pl.ds(hid.shape[0], flat.shape[0])], out_sems.at[1]).wait()
     hidden_copy.wait()
 
 
@@ -207,15 +207,21 @@
         spare, landing = (fin // 8, 8, hid_width), (n, 8, hid_width)
     else:
         spare = landing = (1, 8, 128)
+    out_type = BF16 if pieces else F32
+    hbm = pl.BlockSpec(memory_space=pltpu.HBM)
+    if pieces:
+        spare, landing = (fin // 8, 8, hid_width), (n, 8, hid_width)
+    else:
+        spare = landing = (1, 8, 128)
     grad_type = GRAD_LINK if pieces else F32
     grad_shape = jax.ShapeDtypeStruct((fin, hid_width), grad_type)
     dma = pltpu.SemaphoreType.DMA
-    hidden_shape = jax.ShapeDtypeStruct((nodes, hid_width), F32)
-    hidden, grad = pl.pallas_call(
+    packed_shape = jax.ShapeDtypeStruct((nodes + fin, hid_width), out_type)
+    packed = pl.pallas_call(
         functools.partial(kernel, n_grp, n_blk, pieces),
-        out_shape=(hidden_shape, grad_shape),
+        out_shape=packed_shape,
         in_specs=[hbm] * 8,
-        out_specs=(hbm, hbm),
+        out_specs=hbm,
         scratch_shapes=[
             pltpu.SMEM(tile_cols.shape, jnp.int32),
             pltpu.VMEM((nodes, fin), BF16),
@@ -229,8 +235,8 @@
             pltpu.VMEM((tile, fin), F32),
             pltpu.VMEM((n_blk - 1, tile, fin), BF16),
             pltpu.VMEM((n_blk - 1, tile, fin), BF16),
-            pltpu.VMEM((nodes, hid_width), F32),
-            pltpu.VMEM((fin, hid_width), grad_type),
+            pltpu.VMEM((nodes, hid_width), out_type),
+            pltpu.VMEM((fin, hid_width), out_type),
             pltpu.VMEM(spare, GRAD_LINK),
             pltpu.VMEM(spare, GRAD_LINK),
             pltpu.VMEM(landing, GRAD_LINK),
@@ -241,9 +247,10 @@
             collective_id=0, has_side_effects=True, vmem_limit_bytes=VLIM),
     )(tile_cols, features, col_scale.reshape(1, nodes), row_scale.reshape(1, nodes), tiles, weight,
       cotangent, train_mask.reshape(1, nodes))
+    hidden, grad = packed[:nodes].astype(BF16), packed[nodes:].astype(F32)
     if not pieces:
         grad = lax.psum(grad, ("grp", "blk"))
-    return hidden.astype(BF16), grad.astype(F32)
+    return hidden, grad
 
 
 def solution(mesh):

time: 29.5 us -> 28.9 us (0.980)
  other arithmetic: 2.24 us -> 1.56 us
    convert_element_type x2 -> x1, other arithmetic: 2.24 us -> 1.56 us  [shards(): hidden, grad = (packed[:nodes].astype(BF16), packed[nodes:].astype(F32))]
where the time goes in v4:
time: 28.9 us; the launch traced here: 28.7 us
  Pallas kernels  26.5 us (92%)
  other arithmetic  1.56 us (5%)
  between operations  0.64 us (2%)
    pallas_call x1, Pallas kernels, shards(): pl.pallas_call(functools.partial(kernel, n_grp, n_blk, pieces), out_shape...  26.5 us
    convert_element_type x1, other arithmetic, shards(): hidden, grad = (packed[:nodes].astype(BF16), packed[nodes:].astype(F32))  1.56 us

profile of v4, /device:TPU:0, one launch (start us, length us, event | category | flops | bytes accessed | tf_op | source)
XLA Modules:
  0.0 28.7 jit_solution(730316604987743650)
XLA Ops:
  0.6 26.5 %shard_map.95 = bf16[256,256]{1,0:T(8,128)(2,1)} custom-call(s32[32]{0:T(128)} %cols_in.1, bf16[128,128]{1,0:T(8,128)(2,1)} %features.1, f32[1,128]{1,0:T(1,128)} %bitcast.3, f32[1,128]{1,0:T(1,128)} %bitcast.4, bf16[32,128,128]{2,1,0:T(8,128)(2,1)} %tiles.1, bf16[128,256]{1,0:T(8,128)(2,1)} %weight.1, bf16[128,256]{1,0:T(8,128)(2,1)} %cotangent.1, ...), custom_call_target="tpu_custom_call" | custom-call | tf_op jit(solution)/shard_map/pallas_call | solution.py:220
  27.1 1.6 %slice_convert_fusion = (f32[128,256]{1,0:T(8,128)}, bf16[128,256]{1,0:T(8,128)(2,1)}) fusion(bf16[256,256]{1,0:T(8,128)(2,1)} %shard_map.95), kind=kLoop, calls=%fused_computation | loop fusion | flops 32768 | bytes 327680 | tf_op jit(solution)/shard_map/convert_element_type | solution.py:250

commit v5 on v4

--- a/solution.py
+++ b/solution.py
@@ -181,18 +181,27 @@
             return 0
 
         lax.fori_loop(1, n, gather, 0)
-        pltpu.make_async_copy(some, some, grad_sems.at[0]).wait()
         pltpu.make_async_copy(some, some, grad_sems.at[3]).wait()
-        pltpu.make_async_copy(others, others, grad_sems.at[2]).wait()
 
     @pl.when(jnp.logical_not(owner))
     def _():
-        pltpu.make_async_copy(grad_parts, grad_parts, grad_sems.at[0]).wait()
         pltpu.make_async_copy(grad_parts, grad_parts, grad_sems.at[3]).wait()
 
     for piece in range(owners):
         flat[piece * 8:piece * 8 + 8] = grad_all[piece]
-    load(flat, packed.at[pl.ds(hid.shape[0], flat.shape[0])], out_sems.at[1]).wait()
+    grad_copy = load(flat, packed.at[pl.ds(hid.shape[0], flat.shape[0])], out_sems.at[1])
+
+    @pl.when(owner)
+    def _():
+        others = grad_in.at[pl.ds(0, n - 1)]
+        pltpu.make_async_copy(some, some, grad_sems.at[0]).wait()
+        pltpu.make_async_copy(others, others, grad_sems.at[2]).wait()
+
+    @pl.when(jnp.logical_not(owner))
+    def _():
+        pltpu.make_async_copy(grad_parts, grad_parts, grad_sems.at[0]).wait()
+
+    grad_copy.wait()
     hidden_copy.wait()
 
 

time: 28.9 us -> 28.9 us (level)
  no operation moved by 1% of the time
where the time goes in v5:
time: 28.9 us; the launch traced here: 28.7 us
  Pallas kernels  26.5 us (92%)
  other arithmetic  1.56 us (5%)
  between operations  0.64 us (2%)
    pallas_call x1, Pallas kernels, shards(): pl.pallas_call(functools.partial(kernel, n_grp, n_blk, pieces), out_shape...  26.5 us
    convert_element_type x1, other arithmetic, shards(): hidden, grad = (packed[:nodes].astype(BF16), packed[nodes:].astype(F32))  1.56 us

profile of v5, /device:TPU:0, one launch (start us, length us, event | category | flops | bytes accessed | tf_op | source)
XLA Modules:
  0.0 28.7 jit_solution(9161448668417224116)
XLA Ops:
  0.6 26.5 %shard_map.95 = bf16[256,256]{1,0:T(8,128)(2,1)} custom-call(s32[32]{0:T(128)} %cols_in.1, bf16[128,128]{1,0:T(8,128)(2,1)} %features.1, f32[1,128]{1,0:T(1,128)} %bitcast.3, f32[1,128]{1,0:T(1,128)} %bitcast.4, bf16[32,128,128]{2,1,0:T(8,128)(2,1)} %tiles.1, bf16[128,256]{1,0:T(8,128)(2,1)} %weight.1, bf16[128,256]{1,0:T(8,128)(2,1)} %cotangent.1, ...), custom_call_target="tpu_custom_call" | custom-call | tf_op jit(solution)/shard_map/pallas_call | solution.py:229
  27.1 1.6 %slice_convert_fusion = (f32[128,256]{1,0:T(8,128)}, bf16[128,256]{1,0:T(8,128)(2,1)}) fusion(bf16[256,256]{1,0:T(8,128)(2,1)} %shard_map.95), kind=kLoop, calls=%fused_computation | loop fusion | flops 32768 | bytes 327680 | tf_op jit(solution)/shard_map/convert_element_type | solution.py:259
